TPU v7x, 32 devices: a whole 2x2x4 slice. The times are simulated.
32 devices in a mesh: fsdp: 8 (over z, y), tp: 4 (over x, core).
Axes of the slice: x: 2, y: 2, z: 4, core: 2. Of those that a mesh axis runs over, the one named last changes fastest.
Arguments:
- inputs: bfloat16 [16, 736, 1152], P('fsdp', 'tp'), may hold values from -6 to 6
- cotangent: bfloat16 [16, 736, 1152], P('fsdp', 'tp'), may hold values from -6 to 6
- lengths: int32 [16], P('fsdp'), may hold values from 1 to 729, as said below
- ln1_gain: bfloat16 [1152], P('fsdp'), may hold values from 0.099609375 to 1.8984375
- ln1_bias: bfloat16 [1152], P('fsdp'), may hold values from -0.3125 to 0.3125
- q_weight: bfloat16 [1152, 1152], P('fsdp', 'tp'), may hold values from -0.1875 to 0.1875
- q_bias: bfloat16 [1152], P('tp'), may hold values from -3 to 3
- k_weight: bfloat16 [1152, 1152], P('fsdp', 'tp'), may hold values from -0.1875 to 0.1875
- v_weight: bfloat16 [1152, 1152], P('fsdp', 'tp'), may hold values from -0.1875 to 0.1875
- v_bias: bfloat16 [1152], P('tp'), may hold values from -0.1875 to 0.1875
- out_weight: bfloat16 [1152, 1152], P('tp', 'fsdp'), may hold values from -2.5 to 2.5
- out_bias: bfloat16 [1152], P('fsdp'), may hold values from -1.75 to 1.75
- ln2_gain: bfloat16 [1152], P('fsdp'), may hold values from 0.099609375 to 1.8984375
- ln2_bias: bfloat16 [1152], P('fsdp'), may hold values from -1.75 to 1.75
- up_weight: bfloat16 [1152, 4304], P('fsdp', 'tp'), may hold values from -0.1875 to 0.1875
- up_bias: bfloat16 [4304], P('tp'), may hold values from -1.75 to 1.75
- down_weight: bfloat16 [4304, 1152], P('tp', 'fsdp'), may hold values from -0.09375 to 0.09375
- down_bias: bfloat16 [1152], P('fsdp'), may hold values from -1.75 to 1.75
Outputs:
- layer_out: bfloat16 [16, 736, 1152], P('fsdp', 'tp')
- input_grad: float32 [16, 736, 1152], P('fsdp', 'tp')
- ln1_gain_grad: float32 [1152], P('fsdp')
- ln1_bias_grad: float32 [1152], P('fsdp')
- q_weight_grad: float32 [1152, 1152], P('fsdp', 'tp')
- q_bias_grad: float32 [1152], P('tp')
- k_weight_grad: float32 [1152, 1152], P('fsdp', 'tp')
- v_weight_grad: float32 [1152, 1152], P('fsdp', 'tp')
- v_bias_grad: float32 [1152], P('tp')
- out_weight_grad: float32 [1152, 1152], P('tp', 'fsdp')
- out_bias_grad: float32 [1152], P('fsdp')
- ln2_gain_grad: float32 [1152], P('fsdp')
- ln2_bias_grad: float32 [1152], P('fsdp')
- up_weight_grad: float32 [1152, 4304], P('fsdp', 'tp')
- up_bias_grad: float32 [4304], P('tp')
- down_weight_grad: float32 [4304, 1152], P('tp', 'fsdp')
- down_bias_grad: float32 [1152], P('fsdp')
Inputs may be any that keep to these rules, and one draw needn't show every extreme that they name: `lengths`: each slot either holds one image of 729 tokens or is empty with length 1; exactly 11 slots hold images, which ones drawn from the seed.
All inputs are finite; a program needn't handle non-finite values.
Results may differ from a plain program's by a relative error of at most 0.013.
Values may be sent and summed in bfloat16 or wider, within the bound.
No kernel may reach another device: no remote copies, remote signals or barrier semaphores. Data moves between devices by JAX's collectives and lax.ppermute only.
A program may use at most 192 MiB of HBM per device.

v0:
```python
import functools

import jax
import jax.numpy as jnp
from jax import lax
from jax.experimental import pallas as pl
from jax.experimental.pallas import tpu as pltpu
from jax.sharding import PartitionSpec as P

HD = 72
EPS = 1e-06
BF = jnp.bfloat16
F32 = jnp.float32
LOG2E = 1.4426950408889634
CHUNK = 16
VM = pl.BlockSpec(memory_space=pltpu.VMEM)
SM = pl.BlockSpec(memory_space=pltpu.SMEM)
HBM = pl.BlockSpec(memory_space=pl.ANY)


def dg(a, b, ca, cb):
    return lax.dot_general(a, b, (((ca,), (cb,)), ((), ())), preferred_element_type=F32)


def call(body, name, ins, specs, outs, scratch, flops, exps=0, limit=48):
    shapes = [jax.ShapeDtypeStruct(s, d) for s, d in outs]
    moved = sum(a.size * a.dtype.itemsize for a in ins)
    moved += sum(s.size * s.dtype.itemsize for s in shapes)
    return pl.pallas_call(
        body,
        out_shape=shapes,
        in_specs=specs,
        out_specs=[VM] * len(outs),
        scratch_shapes=scratch,
        compiler_params=pltpu.CompilerParams(vmem_limit_bytes=limit << 20),
        name=name,
        cost_estimate=pl.CostEstimate(
            flops=int(flops), bytes_accessed=int(moved), transcendentals=int(exps)
        ),
    )(*ins)


def staged(body, name, ins, modes, outs, out_modes, scratch, flops, exps=0, limit=44):
    shapes = [jax.ShapeDtypeStruct(s, d) for s, d in outs]
    kinds = {"S": SM, "V": VM}
    buffers, moves = [], 0
    for x, m in zip(ins, modes):
        if m not in ("S", "V", "A"):
            buffers.append(pltpu.VMEM(x.shape if m == "H" else x.shape[1:], x.dtype))
            moves += 1
    for (shape, kind), m in zip(outs, out_modes):
        if m == "H":
            buffers.append(pltpu.VMEM(shape, kind))
            moves += 4
    n_in, n_out, n_own = len(ins), len(outs), len(scratch)

    def kernel(*refs):
        in_refs, out_refs = refs[:n_in], refs[n_in : n_in + n_out]
        own = refs[n_in + n_out : n_in + n_out + n_own]
        spare = list(refs[n_in + n_out + n_own : -1])
        sems = refs[-1]
        used = []

        def copy(src, dst):
            c = pltpu.make_async_copy(src, dst, sems.at[len(used)])
            c.start()
            used.append(c)
            return c

        views, arriving, out_views, leaving = [], {}, [], []
        for i, (ref, m) in enumerate(zip(in_refs, modes)):
            if m in ("S", "V", "A"):
                views.append(ref)
            else:
                buf = spare.pop(0)
                arriving[i] = copy(ref if m == "H" else ref.at[m], buf)
                views.append(buf)
        for ref, m in zip(out_refs, out_modes):
            out_views.append(spare.pop(0) if m == "H" else ref)

        def ready(*which):
            for i in which:
                if i in arriving:
                    arriving.pop(i).wait()

        def leave(o, a, b):
            if out_modes[o] == "H":
                leaving.append(copy(out_views[o].at[a:b], out_refs[o].at[a:b]))

        body(ready, leave, *views, *out_views, *own)
        for c in leaving:
            c.wait()

    moved = sum(a.size * a.dtype.itemsize for a in ins) + sum(
        s.size * s.dtype.itemsize for s in shapes
    )
    return pl.pallas_call(
        kernel,
        out_shape=shapes,
        in_specs=[kinds.get(m, HBM) for m in modes],
        out_specs=[HBM if m == "H" else VM for m in out_modes],
        scratch_shapes=list(scratch) + buffers + [pltpu.SemaphoreType.DMA((max(moves, 1),))],
        compiler_params=pltpu.CompilerParams(vmem_limit_bytes=limit << 20),
        name=name,
        cost_estimate=pl.CostEstimate(
            flops=int(flops), bytes_accessed=int(moved), transcendentals=int(exps)
        ),
    )(*ins)


def normal(x):
    average = jnp.mean(x, -1, keepdims=True)
    center = x - average
    variance = jnp.mean(center * center, -1, keepdims=True)
    inverse = lax.rsqrt(variance + EPS)
    return center * inverse, inverse


def normal_back(hat, inverse, scaled):
    first = jnp.mean(scaled, -1, keepdims=True)
    second = jnp.mean(scaled * hat, -1, keepdims=True)
    return inverse * (scaled - first - hat * second)


def positions(sc_ref, rows, shape, dim):
    r = lax.broadcasted_iota(jnp.int32, shape, dim)
    ti = sc_ref[0]
    p0, p2, p1, p3 = ((ti ^ j) * rows for j in (0, 2, 1, 3))
    return jnp.where(
        r < 2 * rows,
        jnp.where(r < rows, r + p0, r + (p2 - rows)),
        jnp.where(r < 3 * rows, r + (p1 - 2 * rows), r + (p3 - 3 * rows)),
    )


def attn_kernel(heads, rows, slot, sc_ref, xo, xf, xno, xnf, vec_ref, shift_ref, w_ref,
                n1_ref, qkv_ref, mixed_ref, lse_ref, keep_ref, send_ref, s_ref, p_ref):
    seq = 4 * rows
    half = 2 * rows
    hw = heads * HD
    c = LOG2E * HD**-0.5
    gain, bias = vec_ref[0:1, :], vec_ref[1:2, :]
    for i, pair in enumerate(((xo, xf), (xno, xnf))):
        parts = [normal(ref[slot].astype(F32))[0] * gain + bias for ref in pair]
        n1 = jnp.concatenate(parts, 0).astype(BF)
        n1_ref[i * half : (i + 1) * half, :] = n1
        qkv_ref[i * half : (i + 1) * half, :] = (dg(n1, w_ref[...], 1, 0) + shift_ref[...]).astype(BF)
    lane = lax.broadcasted_iota(jnp.int32, (seq, 128), 1)
    pos = positions(sc_ref, rows, (seq, 128), 0)
    mask = jnp.where((lane == HD) & (pos >= sc_ref[1]), -1e30, 0.0).astype(BF)
    one = jnp.where(lane == HD, 1.0, 0.0).astype(BF)
    for h in range(heads):
        a = hw + HD * h
        qx = jnp.where(lane < HD, qkv_ref[:, a : a + 128], one)
        kx = jnp.where(lane < HD, qkv_ref[:, hw + a : hw + a + 128], mask)
        v = qkv_ref[:, 2 * hw + a : 2 * hw + a + HD]
        sl = h % 2
        s_ref[sl] = dg(kx, qx, 1, 1)
        m = s_ref[sl, 0:CHUNK, :]
        for r in range(CHUNK, seq, CHUNK):
            m = jnp.maximum(m, s_ref[sl, r : r + CHUNK, :])
        m = jnp.max(m, 0, keepdims=True) * c
        total = jnp.zeros((CHUNK, seq), F32)
        for r in range(0, seq, CHUNK):
            p = jnp.exp2(s_ref[sl, r : r + CHUNK, :] * c - m)
            total = total + p
            p_ref[sl, r : r + CHUNK, :] = p.astype(BF)
        total = jnp.sum(total, 0, keepdims=True)
        lse_ref[h : h + 1, :] = m + jnp.log2(total)
        mixed = dg(v, p_ref[sl], 0, 0) * (1.0 / total)
        mixed_ref[:, HD * h : HD * h + HD] = mixed.T.astype(BF)
    for i, ref in enumerate((keep_ref, send_ref)):
        ref[...] = dg(mixed_ref[i * half : (i + 1) * half, :], w_ref[:, 0:hw], 1, 1).astype(BF)


def attn(s, sc, blocks, vec, shift, w):
    rows, width = blocks[0].shape[1:]
    seq, hw = 4 * rows, w.shape[1] // 4
    heads = hw // HD
    ins = (sc, *blocks, vec, shift, w)
    outs = [((seq, width), BF), ((seq, 4 * hw), BF), ((seq, hw), BF), ((8, seq), F32)]
    outs += [((2 * rows, width), BF)] * 2
    return call(
        functools.partial(attn_kernel, heads, rows, s), "attn_fwd", ins,
        [SM] + [VM] * 7, outs,
        [pltpu.VMEM((2, seq, seq), F32), pltpu.VMEM((2, seq, seq), BF)],
        2 * seq * width * 5 * hw + 16 * seq * seq * 128 * heads, heads * seq * seq, limit=20,
    )


def attn_back_kernel(heads, rows, sc_ref, ga_ref, gb_ref, w_ref, qkv_ref, lse_ref,
                     gq_ref, keep_ref, send_ref, col_ref, s_ref, g_ref, p_ref, d_ref, gm_ref):
    seq = 4 * rows
    half = 2 * rows
    hw = heads * HD
    scale = HD**-0.5
    c = LOG2E * scale
    for i, ref in enumerate((ga_ref, gb_ref)):
        gm_ref[i * half : (i + 1) * half, :] = dg(ref[...], w_ref[:, 0:hw], 1, 0).astype(BF)
    lane = lax.broadcasted_iota(jnp.int32, (seq, 128), 1)
    pos = positions(sc_ref, rows, (seq, 128), 0)
    mask = jnp.where((lane == HD) & (pos >= sc_ref[1]), -1e30, 0.0).astype(BF)
    one = jnp.where(lane == HD, 1.0, 0.0).astype(BF)
    gq_ref[:, 0:hw] = jnp.zeros((seq, hw), BF)
    for h in range(heads):
        a = hw + HD * h
        qx = jnp.where(lane < HD, qkv_ref[:, a : a + 128], one)
        kx = jnp.where(lane < HD, qkv_ref[:, hw + a : hw + a + 128], mask)
        q = qkv_ref[:, a : a + HD]
        k = qkv_ref[:, hw + a : hw + a + HD]
        v = qkv_ref[:, 2 * hw + a : 2 * hw + a + HD]
        g = gm_ref[:, HD * h : HD * h + HD]
        sl = h % 2
        s_ref[sl] = dg(kx, qx, 1, 1)
        g_ref[sl] = dg(v, g, 1, 1)
        lse = lse_ref[h : h + 1, :]
        inner = jnp.zeros((CHUNK, seq), F32)
        for r in range(0, seq, CHUNK):
            p = jnp.exp2(s_ref[sl, r : r + CHUNK, :] * c - lse)
            s_ref[sl, r : r + CHUNK, :] = p
            p_ref[sl, r : r + CHUNK, :] = p.astype(BF)
            inner = inner + p * g_ref[sl, r : r + CHUNK, :]
        inner = jnp.sum(inner, 0, keepdims=True)
        for r in range(0, seq, CHUNK):
            d_ref[sl, r : r + CHUNK, :] = (
                s_ref[sl, r : r + CHUNK, :] * (g_ref[sl, r : r + CHUNK, :] - inner)
            ).astype(BF)
        gq_ref[:, a : a + HD] = (dg(k, d_ref[sl], 0, 0) * scale).T.astype(BF)
        gq_ref[:, hw + a : hw + a + HD] = (dg(d_ref[sl], q, 1, 0) * scale).astype(BF)
        gq_ref[:, 2 * hw + a : 2 * hw + a + HD] = dg(p_ref[sl], g, 1, 0).astype(BF)
    col = None
    for i, ref in enumerate((keep_ref, send_ref)):
        part = gq_ref[i * half : (i + 1) * half, :]
        ref[...] = dg(part, w_ref[...], 1, 1).astype(BF)
        now = jnp.sum(part.astype(F32), 0, keepdims=True)
        col = now if col is None else col + now
    col_ref[...] = col


def attn_back(sc, gml, w, qkv, lse):
    half, width = gml[0].shape
    seq, hw = 2 * half, w.shape[1] // 4
    heads = hw // HD
    ins = (sc, *gml, w, qkv, lse)
    outs = [((seq, 4 * hw), BF), ((half, width), BF), ((half, width), BF), ((1, 4 * hw), F32)]
    return call(
        functools.partial(attn_back_kernel, heads, half // 2), "attn_bwd", ins,
        [SM] + [VM] * 5, outs,
        [pltpu.VMEM((2, seq, seq), F32)] * 2 + [pltpu.VMEM((2, seq, seq), BF)] * 2
        + [pltpu.VMEM((seq, hw), BF)],
        2 * seq * width * 5 * hw + 24 * seq * seq * 128 * heads, heads * seq * seq, limit=30,
    )


def mlp_kernel(rows, slot, sc_ref, na_ref, nb_ref, co, cf, cno, cnf, w_ref, ub_ref,
               act_ref, gh_ref, go_ref, okeep_ref, osend_ref, gkeep_ref, gsend_ref, us_ref):
    half = 2 * rows
    c0 = 0.7978845608028654
    limit = sc_ref[1]
    us = None
    units = ub_ref.shape[1]
    main = units - units % 128
    wu_ref = w_ref.at[:, 0:units]
    wa_ref, wb_ref = w_ref.at[:, main + 128 :], w_ref.at[:, units : 2 * units - main]
    for i, (n_ref, pair, o_ref, g_ref) in enumerate((
        (na_ref, (co, cf), okeep_ref, gkeep_ref),
        (nb_ref, (cno, cnf), osend_ref, gsend_ref),
    )):
        parts = []
        for j, ref in enumerate(pair):
            start = (sc_ref[0] ^ ((0, 2, 1, 3)[2 * i + j])) * rows
            pos = lax.broadcasted_iota(jnp.int32, ref.shape[1:], 0) + start
            parts.append(jnp.where(pos < limit, ref[slot].astype(F32), 0.0))
        go = jnp.concatenate(parts, 0).astype(BF)
        go_ref[i * half : (i + 1) * half, :] = go
        hidden = dg(n_ref[...], wu_ref[...], 1, 0) + ub_ref[...]
        square = hidden * hidden
        t = jnp.tanh(hidden * (c0 + (c0 * 0.044715) * square))
        act = (0.5 * hidden * (1.0 + t)).astype(BF)
        slope = 0.5 * (1.0 + t) + hidden * (1.0 - t * t) * (0.5 * c0 + (1.5 * c0 * 0.044715) * square)
        act_ref[i * half : (i + 1) * half, :] = act
        o_ref[...] = (
            dg(act[:, 0:main], wa_ref[...], 1, 1) + dg(act[:, main:], wb_ref[...], 1, 1)
        ).astype(BF)
        grad = jnp.concatenate([dg(go, wa_ref[...], 1, 0), dg(go, wb_ref[...], 1, 0)], 1)
        gh = (grad * slope).astype(BF)
        gh_ref[i * half : (i + 1) * half, :] = gh
        g_ref[...] = dg(gh, wu_ref[...], 1, 1).astype(BF)
        now = jnp.sum(gh.astype(F32), 0, keepdims=True)
        us = now if us is None else us + now
    us_ref[...] = us


def mlp(s, sc, n2, blocks, w, ub):
    half, width = n2[0].shape
    rows, seq, units = half // 2, 2 * half, ub.shape[1]
    ins = (sc, *n2, *blocks, w, ub)
    outs = [((seq, units), BF), ((seq, units), BF), ((seq, width), BF)]
    outs += [((half, width), BF)] * 4 + [((1, units), F32)]
    return call(
        functools.partial(mlp_kernel, rows, s), "mlp", ins,
        [SM] + [VM] * 8, outs, [],
        8 * seq * width * units, seq * units, limit=22,
    )


def pair_kernel(n, plan, pad, *refs):
    ins, out = refs[:n], refs[n]
    depth = out.shape[0]
    step = 384 if depth % 384 == 0 else depth
    for at, pairs in plan:
        for a in range(0, depth, step):
            total = None
            for l, r, first in pairs:
                right = ins[r][first : first + ins[l].shape[0], :]
                now = dg(ins[l][:, a : a + step], right, 0, 0)
                total = now if total is None else total + now
            if pad:
                fill = (-total.shape[1]) % 128
                total = jnp.concatenate([total, jnp.zeros((step, fill), F32)], 1)
            out[a : a + step, at : at + total.shape[1]] = total.astype(BF)


def weight_sums(name, depth, width, plan, pad=False, limit=23):
    ins, table, out, flops = [], {}, [], 0

    def index(x):
        if id(x) not in table:
            table[id(x)] = len(ins)
            ins.append(x)
        return table[id(x)]

    for at, pairs in plan:
        out.append((at, [(index(l), index(r), first) for l, r, first in pairs]))
        flops += sum(2 * l.shape[0] * l.shape[1] * r.shape[1] for l, r, _ in pairs)
    return call(
        functools.partial(pair_kernel, len(ins), out, pad), name, tuple(ins), [VM] * len(ins),
        [((depth, width), BF)], [], flops, limit=limit,
    )[0]


def mlp_sums_kernel(rows, n2a0, n2b0, n2a1, n2b1, gh0, gh1, go0, go1, act0, act1, out):
    depth, units = out.shape[0], act0.shape[1]
    main = units - units % 128
    step = 384 if depth % 384 == 0 else depth
    for a in range(0, depth, step):
        cut = slice(a, a + step)
        up = None
        for na, nb, gh in ((n2a0, n2b0, gh0), (n2a1, n2b1, gh1)):
            now = dg(na[:, cut], gh[0:rows, :], 0, 0) + dg(nb[:, cut], gh[rows:, :], 0, 0)
            up = now if up is None else up + now
        last = dg(go0[:, cut], act0[:, main:], 0, 0) + dg(go1[:, cut], act1[:, main:], 0, 0)
        fill = jnp.zeros((step, 128 - 2 * (units - main)), F32)
        out[cut, 0 : main + 128] = jnp.concatenate([up, last, fill], 1).astype(BF)
        out[cut, main + 128 :] = (
            dg(go0[:, cut], act0[:, 0:main], 0, 0) + dg(go1[:, cut], act1[:, 0:main], 0, 0)
        ).astype(BF)


def mlp_sums(n2s, ghs, gos, acts, packed):
    rows, width = n2s[0][0].shape
    ins = (*n2s[0], *n2s[1], *ghs, *gos, *acts)
    return call(
        functools.partial(mlp_sums_kernel, rows), "mlp_dw", ins, [VM] * 10, [((width, packed), BF)], [],
        16 * rows * width * acts[0].shape[1], limit=23,
    )[0]


def middle_kernel(rows, slot, xo, xf, chip_ref, far_ref, vec_ref, mid_ref, n2_ref):
    parts = []
    for i, ref in enumerate((xo, xf)):
        a, b = i * rows, (1 - i) * rows
        mid = ref[slot].astype(F32) + (
            chip_ref[a : a + rows, :].astype(F32) + far_ref[b : b + rows, :].astype(F32)
        ) + vec_ref[2:3, :]
        mid_ref[a : a + rows, :] = mid
        parts.append(normal(mid)[0] * vec_ref[3:4, :] + vec_ref[4:5, :])
    n2_ref[...] = jnp.concatenate(parts, 0).astype(BF)


def middle_norm(s, xo, xf, chip, far, vec):
    half, width = chip.shape
    rows = half // 2
    return call(
        functools.partial(middle_kernel, rows, s), "middle_norm", (xo, xf, chip, far, vec),
        [VM] * 5, [((half, width), F32), ((half, width), BF)], [], 20 * half * width, limit=5,
    )


def middle_back_kernel(rows, slot, sc_ref, co, cf, chip_ref, far_ref, mid_ref, vec_ref, gm_ref, gml_ref, sum_ref):
    parts = []
    for i, ref in enumerate((co, cf)):
        a, b = i * rows, (1 - i) * rows
        pos = lax.broadcasted_iota(jnp.int32, ref.shape[1:], 0) + (sc_ref[0] ^ (2 * i)) * rows
        go = jnp.where(pos < sc_ref[1], ref[slot].astype(F32), 0.0)
        grad = chip_ref[a : a + rows, :].astype(F32) + far_ref[b : b + rows, :].astype(F32)
        hat, inverse = normal(mid_ref[a : a + rows, :])
        gm = go + normal_back(hat, inverse, grad * vec_ref[3:4, :])
        parts.append(gm)
        if i == 0:
            gm_ref[...] = gm
            sum_ref[0:1, :] = jnp.sum(gm, 0, keepdims=True)
            sum_ref[1:2, :] = jnp.sum(hat * grad, 0, keepdims=True)
            sum_ref[2:3, :] = jnp.sum(grad, 0, keepdims=True)
            sum_ref[3:4, :] = jnp.sum(go, 0, keepdims=True)
    gml_ref[...] = jnp.concatenate(parts, 0).astype(BF)


def middle_back(s, sc, co, cf, chip, far, mid, vec):
    half, width = chip.shape
    rows = half // 2
    return call(
        functools.partial(middle_back_kernel, rows, s), "middle_bwd", (sc, co, cf, chip, far, mid, vec),
        [SM] + [VM] * 6,
        [((rows, width), F32), ((half, width), BF), ((4, width), F32)], [], 40 * half * width, limit=10,
    )


def input_back_kernel(rows, slot, xo, keep_ref, near_ref, far_ref, gm_ref, vec_ref, out_ref, sum_ref):
    grad = (
        keep_ref[0:rows, :].astype(F32) + near_ref[0:rows, :].astype(F32) + far_ref[...].astype(F32)
    )
    hat, inverse = normal(xo[slot].astype(F32))
    out_ref[...] = gm_ref[...] + normal_back(hat, inverse, grad * vec_ref[0:1, :])
    sum_ref[0:1, :] = jnp.sum(hat * grad, 0, keepdims=True)
    sum_ref[1:2, :] = jnp.sum(grad, 0, keepdims=True)


def input_back(s, xo, keep, near, far, gm, vec):
    rows, width = far.shape
    return call(
        functools.partial(input_back_kernel, rows, s), "input_bwd", (xo, keep, near, far, gm, vec),
        [VM] * 6, [((rows, width), F32), ((2, width), F32)], [],
        30 * rows * width, limit=5,
    )


def pack_attn_kernel(*refs):
    ins, out_ref, held, lines, sems = refs[:10], refs[10], refs[11:15], refs[15:21], refs[21]
    copies = [
        pltpu.make_async_copy(src, dst, sems.at[i]) for i, (src, dst) in enumerate(zip(ins, held + lines))
    ]
    for copy in copies:
        copy.start()
    for copy in copies:
        copy.wait()
    shard, hw = held[0].shape
    out_ref[0:shard, 0:hw] = held[3][...].astype(F32).T.astype(BF)
    for i in range(3):
        out_ref[0:shard, (i + 1) * hw : (i + 2) * hw] = held[i][...]
    rows = [ref[...].astype(F32).reshape(1, shard) for ref in lines]
    rows = jnp.concatenate(rows + [jnp.zeros((2, shard), F32)], 0)
    rows = jnp.concatenate([rows, jnp.zeros((8, 4 * hw - shard), F32)], 1)
    out_ref[shard : shard + 8, :] = rows.astype(BF)


def pack_mlp_kernel(ready, leave, u_ref, d_ref, out_ref):
    ready(0, 1)
    shard, units = u_ref.shape
    main = units - units % 128
    down = d_ref[...].astype(F32).T
    fill = jnp.zeros((shard, 128 - 2 * (units - main)), F32)
    out_ref[:, 0 : main + 128] = jnp.concatenate(
        [u_ref[...].astype(F32), down[:, main:], fill], 1
    ).astype(BF)
    out_ref[:, main + 128 :] = down[:, 0:main].astype(BF)


def place_kernel(n, cuts, idx_ref, *refs):
    sources, outs, sems = refs[:n], refs[n:-1], refs[-1]
    copies = []
    for i, src in enumerate(sources):
        for o, (a, b) in enumerate(cuts):
            dst = outs[o].at[idx_ref[i]]
            copies.append(pltpu.make_async_copy(src.at[a:b], dst, sems.at[len(copies)]))
    for c in copies:
        c.start()
    for c in copies:
        c.wait()


def place_shards(idx, sources, cuts):
    n = len(sources)
    cols = sources[0].shape[1]
    outs = [((n, b - a, cols), BF) for a, b in cuts]
    return call(
        functools.partial(place_kernel, n, cuts), "place_shards", (idx, *sources), [SM] + [HBM] * n,
        outs, [pltpu.SemaphoreType.DMA((n * len(cuts),))], 0, limit=6,
    )


def close_kernel(n, *refs):
    total = refs[0][...].astype(F32)
    for ref in refs[1:n]:
        total = total + ref[...].astype(F32)
    hw = total.shape[1] // 4
    for i in range(3):
        refs[n + i][...] = total[:, (i + 1) * hw : (i + 2) * hw]
    refs[n + 3][...] = total[:, 0:hw].T


def close_sums(parts, hw):
    rows, n = parts[0].shape[0], len(parts)
    return call(
        functools.partial(close_kernel, n), "close_sums", tuple(parts), [VM] * n,
        [((rows, hw), F32)] * 3 + [((hw, rows), F32)], [], 8 * rows * hw * n, limit=8,
    )


def after(x, *others):
    return lax.optimization_barrier((x, *others))[0]


def local(
    inputs,
    cotangent,
    lengths,
    ln1_gain,
    ln1_bias,
    q_weight,
    q_bias,
    k_weight,
    v_weight,
    v_bias,
    out_weight,
    out_bias,
    ln2_gain,
    ln2_bias,
    up_weight,
    up_bias,
    down_weight,
    down_bias,
):
    tp = lax.axis_size("tp")
    fs = lax.axis_size("fsdp")
    ti = lax.axis_index("tp")
    fi = lax.axis_index("fsdp")
    slots, rows, width = inputs.shape
    half = 2 * rows
    hw = q_weight.shape[1]
    units = up_weight.shape[1]
    shard = width // fs
    zi, yi = fi // 2, fi % 2

    def swap_tp(x, k):
        return lax.ppermute(x, "tp", [(i, i ^ k) for i in range(tp)])

    def swap_fs(x, k):
        return lax.ppermute(x, "fsdp", [(i, i ^ k) for i in range(fs)])

    def turn(x, k):
        return lax.ppermute(x, "fsdp", [(i, (i + 2 * k) % fs) for i in range(fs)])

    def gather_shards(own, cuts, beside, later):
        if fs != 8:
            whole = lax.all_gather(own, "fsdp", axis=0)
            return tuple(whole[:, a:b] for a, b in cuts), beside(own), later(own), whole
        first = lax.optimization_barrier((turn(own, 1), turn(own, 3), swap_fs(own, 1), beside(own)))
        r1, r3, o0, extra = first
        own, r1, r3, extra = lax.optimization_barrier((own, r1, r3, extra))
        second = (turn(own, 2), swap_fs(r1, 1), swap_fs(r3, 1), later(extra))
        r2, o1, o3, extra2 = lax.optimization_barrier(second)
        o2 = swap_fs(r2, 1)
        order = jnp.stack([(zi + 4 - k) % 4 for k in (0, 1, 3, 2)]) * 2
        idx = jnp.concatenate([order + yi, order + 1 - yi]).astype(jnp.int32)
        sources = [own, r1, r3, r2, o0, o1, o3, o2]
        return place_shards(idx, sources, cuts), extra, extra2, r1

    def scatter_sums(total, beside):
        if fs != 8:
            return [lax.psum_scatter(total, "fsdp", scatter_dimension=0, tiled=True)], beside
        cols = total.shape[1]
        parts = total.reshape(4, 2, shard, cols)

        def pick(k, y):
            return lax.dynamic_slice(parts, ((zi + k) % 4, y, 0, 0), (1, 1, shard, cols))[0, 0]

        first = swap_fs(jnp.stack([pick(k, 1 - yi) for k in (1, 3, 2)], 0), 1)
        mine = swap_fs(pick(0, 1 - yi), 1)
        sums = [(pick(k, yi).astype(F32) + first[j].astype(F32)).astype(BF) for j, k in enumerate((1, 3, 2))]
        *sums, beside = lax.optimization_barrier((*sums, beside))
        got = [turn(a, k) for a, k in zip(sums, (1, 3, 2))]
        return [pick(0, yi), mine, *got], beside

    def chip_sum(keep, send):
        return (keep.astype(F32) + swap_tp(send, 1).astype(F32)).astype(BF)

    def own_part(keep, send):
        near = swap_tp(send, 1)
        far = (keep[rows:].astype(F32) + near[rows:].astype(F32)).astype(BF)
        return near, swap_tp(far, 2)

    shards = (q_weight, k_weight, v_weight, out_weight)
    lines = (ln1_gain, ln1_bias, out_bias, ln2_gain, ln2_bias, down_bias)
    pack = call(
        pack_attn_kernel, "pack_attn", (*shards, *lines), [HBM] * 10, [((shard + 8, 4 * hw), BF)],
        [pltpu.VMEM(a.shape, BF) for a in shards + lines] + [pltpu.SemaphoreType.DMA((10,))], 0, limit=60,
    )[0]
    (w_attn, small), x_far, c_far, sent = gather_shards(
        pack,
        ((0, shard), (shard, shard + 8)),
        lambda _: swap_tp(inputs, 2),
        lambda x: swap_tp(after(cotangent, x), 2),
    )
    x_blocks = (inputs, x_far, swap_tp(inputs, 1), swap_tp(x_far, 1))
    c_blocks = (cotangent, c_far, swap_tp(cotangent, 1), swap_tp(c_far, 1))
    w_attn = w_attn.reshape(width, 4 * hw)
    vec = small[:, :, :shard].transpose(1, 0, 2).reshape(8, width).astype(F32)
    main = units - units % 128
    packed = 2 * main + 128
    pack = staged(
        pack_mlp_kernel, "pack_mlp", (up_weight, down_weight), ["H", "H"], [((shard, packed), BF)],
        ["V"], [], 0, limit=60
    )[0]
    w_mlp = lax.all_gather(after(pack, sent), "fsdp", axis=0, tiled=True)

    none = jnp.zeros_like(q_bias)
    shift = jnp.concatenate([none, q_bias, none, v_bias], 0).astype(F32)[None, :]
    ub = up_bias.astype(F32)[None, :]
    scalars = [jnp.stack([ti, lengths[s]]).astype(jnp.int32) for s in range(slots)]

    every = range(slots)
    fwd, chips, mids, mlps = [], [], [], []
    w_now, fars = w_attn, []
    for s in every:
        fwd.append(attn(s, scalars[s], x_blocks, vec, shift, w_now))
        keep, send = fwd[s][4:6]
        if s == 1:
            fars[0], send = lax.optimization_barrier((fars[0], send))
        chip = chip_sum(keep, send)
        if s < slots - 1:
            chip, w_now = lax.optimization_barrier((chip, w_now))
        chips.append(chip)
        fars.append(swap_tp(chip, 2))
    for s in every:
        far = fars[s]
        if s == 0:
            far, w_mlp = lax.optimization_barrier((far, w_mlp))
        mid, n2 = middle_norm(s, x_blocks[0], x_blocks[1], chips[s], far, vec)
        mids.append((mid, (n2, swap_tp(n2, 1))))
    chips = []
    w_now = w_mlp
    for s in every:
        mlps.append(mlp(s, scalars[s], mids[s][1], c_blocks, w_now, ub))
        chip = chip_sum(mlps[s][5], mlps[s][6])
        if s < slots - 1:
            chip, w_now = lax.optimization_barrier((chip, w_now))
        chips.append(chip)
    fars = [swap_tp(c, 2) for c in chips]
    acts = [m[0] for m in mlps]
    acts[0], fars[0] = lax.optimization_barrier((acts[0], fars[0]))
    g_mlp = mlp_sums([m[1] for m in mids], [m[1] for m in mlps], [m[2] for m in mlps], acts, packed)
    r_mlp = lax.psum_scatter(g_mlp, "fsdp", scatter_dimension=0, tiled=True).astype(F32)
    outs, grads_x = [], []
    wide = cols = None
    heads_out, heads_in = [], []
    mid_now = [m[0] for m in mids]
    for s in every:
        okeep, osend = mlps[s][3:5]
        gm, gml, sums = middle_back(
            s, scalars[s], c_blocks[0], c_blocks[1], chips[s], fars[s], mid_now[s], vec
        )
        gml = (gml, swap_tp(gml, 1))
        n1, qkv, mixed, lse = fwd[s][:4]
        gqkv, keep, send, col = attn_back(scalars[s], gml, w_attn, qkv, lse)
        if s < slots - 1:
            mid_now[s + 1], col = lax.optimization_barrier((mid_now[s + 1], col))
        near, far = own_part(keep, send)
        grad, sums1 = input_back(s, x_blocks[0], keep, near, far, gm, vec)
        grads_x.append(grad)
        near, far = own_part(okeep, osend)
        outs.append(
            (
                mids[s][0][:rows]
                + (okeep[:rows].astype(F32) + near[:rows].astype(F32) + far.astype(F32))
                + vec[5:6]
            ).astype(BF)
        )
        now = jnp.concatenate([sums1, sums], 0)
        wide = now if wide is None else wide + now
        cols = col if cols is None else cols + col
        heads_out += [(gml[i], mixed, i * half) for i in range(2)]
        heads_in.append((n1, gqkv, 0))
    g_attn = weight_sums("attn_dw", width, 4 * hw, [(0, heads_in), (0, heads_out)])

    unit_sums = sum(m[7] for m in mlps)
    wide = wide + swap_tp(wide, 1)
    wide = wide + swap_tp(wide, 2)
    flat = jnp.concatenate(
        [wide.reshape(-1), cols[0, hw : 2 * hw], cols[0, 3 * hw :], unit_sums[0]], 0
    )
    step = 1
    while step < fs:
        flat = flat + swap_fs(flat, step)
        step *= 2
    parts, flat = scatter_sums(g_attn, flat)
    r_up = r_mlp[:, :units]
    r_down = jnp.concatenate([r_mlp[:, main + 128 :], r_mlp[:, units : 2 * units - main]], 1).T
    parts, r_up, r_down = lax.optimization_barrier((parts, r_up, r_down))
    gq, gk, gv, go = close_sums(parts, hw)
    wide = flat[: 6 * width].reshape(6, width)
    wide = lax.dynamic_slice_in_dim(wide, fi * shard, shard, 1)
    tail = flat[6 * width :]
    return (
        jnp.stack(outs, 0),
        jnp.stack(grads_x, 0),
        wide[0],
        wide[1],
        gq,
        tail[:hw],
        gk,
        gv,
        tail[hw : 2 * hw],
        go,
        wide[2],
        wide[3],
        wide[4],
        r_up,
        tail[2 * hw :],
        r_down,
        wide[5],
    )


def solution(mesh):
    rowed = P("fsdp", "tp", None)
    wide = P("fsdp")
    cols = P("fsdp", "tp")
    turned = P("tp", "fsdp")
    part = P("tp")
    in_specs = (
        rowed, rowed, wide, wide, wide, cols, part, cols, cols, part, turned, wide,
        wide, wide, cols, part, turned, wide,
    )
    out_specs = (
        rowed, rowed, wide, wide, cols, part, cols, cols, part, turned, wide, wide, wide,
        cols, part, turned, wide,
    )
    return jax.shard_map(local, mesh=mesh, in_specs=in_specs, out_specs=out_specs, check_vma=False)
```

profile of v0, /device:TPU:0, one launch (start us, length us, event | category | flops | bytes accessed | tf_op | source)
XLA Modules:
  0.0 335.5 jit_solution(12863539175893546664)
XLA Ops:
  7.2 3.0 collective-permute-start.3
  23.8 3.5 %collective-permute-done.refs_1_ = bf16[152,1152]{1,0:T(8,128)(2,1)S(1)} collective-permute-done((bf16[152,1152]{1,0:T(8,128)(2,1)}, bf16[152,1152]{1,0:T(8,128)(2,1)S(1)}, u32[]{:S(2)}, u32[]{:S(2)}) %collective-permute-start) | collective-permute-done | bytes 350240 | tf_op jit(solution)/shard_map/ppermute | solution.py:552
  27.4 5.6 %collective-permute-done.1.refs_2_ = bf16[152,1152]{1,0:T(8,128)(2,1)} collective-permute-done((bf16[152,1152]{1,0:T(8,128)(2,1)}, bf16[152,1152]{1,0:T(8,128)(2,1)}, u32[]{:S(2)}, u32[]{:S(2)}) %collective-permute-start.1) | collective-permute-done | bytes 350240 | tf_op jit(solution)/shard_map/ppermute | solution.py:552
  36.9 32.0 %collective-permute-done.6.refs_3_ = bf16[152,1152]{1,0:T(8,128)(2,1)} collective-permute-done((bf16[152,1152]{1,0:T(8,128)(2,1)S(1)}, bf16[152,1152]{1,0:T(8,128)(2,1)}, u32[]{:S(2)}, u32[]{:S(2)}) %collective-permute-start.6) | collective-permute-done | bytes 350240 | tf_op jit(solution)/shard_map/ppermute | solution.py:552
  72.8 9.2 %collective-permute-done.10.refs_7_ = bf16[152,1152]{1,0:T(8,128)(2,1)} collective-permute-done((bf16[152,1152]{1,0:T(8,128)(2,1)}, bf16[152,1152]{1,0:T(8,128)(2,1)}, u32[]{:S(2)}, u32[]{:S(2)}) %collective-permute-start.10) | collective-permute-done | bytes 350240 | tf_op jit(solution)/shard_map/ppermute | solution.py:549
  88.2 9.7 %attn_fwd.2 = (bf16[736,1152]{1,0:T(8,128)(2,1)S(1)}, bf16[736,1152]{1,0:T(8,128)(2,1)S(1)}, bf16[736,288]{1,0:T(8,128)(2,1)S(1)}, f32[8,736]{1,0:T(8,128)S(1)},...) custom-call(s32[2]{0:T(128)S(1)} %get-tuple-element.244.sc_ref, bf16[2,184,1152]{2,1,0:T(8,128)(2,1)S(1)} %copy-done, ...), custom_call_target="tpu_custom_call" | custom-call | flops 6879444992 | bytes 11621896 | tf_op jit(solution)/shard_map/attn_fwd/pallas_call | solution.py:29
  102.0 10.6 %attn_fwd.3 = (bf16[736,1152]{1,0:T(8,128)(2,1)S(1)}, bf16[736,1152]{1,0:T(8,128)(2,1)S(1)}, bf16[736,288]{1,0:T(8,128)(2,1)S(1)}, f32[8,736]{1,0:T(8,128)S(1)},...) custom-call(s32[2]{0:T(128)S(1)} %get-tuple-element.245.sc_ref, bf16[2,184,1152]{2,1,0:T(8,128)(2,1)S(1)} %copy-done, ...), custom_call_target="tpu_custom_call" | custom-call | flops 6879444992 | bytes 11621896 | tf_op jit(solution)/shard_map/attn_fwd/pallas_call | solution.py:29
  116.8 4.8 %collective-permute-done.12.far_ref = bf16[368,1152]{1,0:T(8,128)(2,1)S(1)} collective-permute-done((bf16[368,1152]{1,0:T(8,128)(2,1)S(1)}, bf16[368,1152]{1,0:T(8,128)(2,1)S(1)}, u32[]{:S(2)}, u32[]{:S(2)}) %collective-permute-start.12) | collective-permute-done | bytes 847904 | tf_op jit(solution)/shard_map/ppermute | solution.py:546
  131.0 13.0 %mlp.2 = (bf16[736,1076]{1,0:T(8,128)(2,1)S(1)}, bf16[736,1076]{1,0:T(8,128)(2,1)S(1)}, bf16[736,1152]{1,0:T(8,128)(2,1)S(1)}, bf16[368,1152]{1,0:T(8,128)(2,1)S...) custom-call(s32[2]{0:T(128)S(1)} %get-tuple-element.244.sc_ref, ...), custom_call_target="tpu_custom_call" | custom-call | flops 7298482176 | bytes 18364328 | tf_op jit(solution)/shard_map/mlp/pallas_call | solution.py:29
  144.2 6.7 %collective-permute-done.19.far_ref = bf16[368,1152]{1,0:T(8,128)(2,1)S(1)} collective-permute-done((bf16[368,1152]{1,0:T(8,128)(2,1)S(1)}, bf16[368,1152]{1,0:T(8,128)(2,1)S(1)}, u32[]{:S(2)}, u32[]{:S(2)}) %collective-permute-start.19) | collective-permute-done | bytes 847904 | tf_op jit(solution)/shard_map/ppermute | solution.py:546
  155.3 12.8 %mlp.3 = (bf16[736,1076]{1,0:T(8,128)(2,1)S(1)}, bf16[736,1076]{1,0:T(8,128)(2,1)S(1)}, bf16[736,1152]{1,0:T(8,128)(2,1)S(1)}, bf16[368,1152]{1,0:T(8,128)(2,1)S...) custom-call(s32[2]{0:T(128)S(1)} %get-tuple-element.245.sc_ref, ...), custom_call_target="tpu_custom_call" | custom-call | flops 7298482176 | bytes 18364328 | tf_op jit(solution)/shard_map/mlp/pallas_call | solution.py:29
  175.4 11.0 %mlp_dw.1 = bf16[1152,2176]{1,0:T(8,128)(2,1)S(1)} custom-call(bf16[368,1152]{1,0:T(8,128)(2,1)S(1)} %get-tuple-element.133.na_ref.n2a0, bf16[368,1152]{1,0:T(8,128)(2,1)S(1)} %collective-permute-done.13.nb_ref.n2b0, bf16[368,1152]{1,0:T(8,128)(2,1)S(1)} %get-tuple-element.141.na_ref.n2a1, bf16[368,1152]{1,0:T(8,128)(2,1)S(1)} %collective-permute-done.20.nb_ref.n2b1, ...), custom_call_target="tpu_custom_call" | custom-call | flops 7298482176 | bytes 18131968 | tf_op jit(solution)/shard_map/mlp_dw/pallas_call | solution.py:29
  191.1 3.5 %middle_bwd.2 = (f32[184,1152]{1,0:T(8,128)S(1)}, bf16[368,1152]{1,0:T(8,128)(2,1)}, f32[4,1152]{1,0:T(4,128)S(1)}) custom-call(s32[2]{0:T(128)S(1)} %get-tuple-element.244.sc_ref, bf16[2,184,1152]{2,1,0:T(8,128)(2,1)S(1)} %copy-done.4, bf16[2,184,1152]{2,1,0:T(8,128)(2,1)} %collective-permute-done.9.cf, bf16[368,1152]{1,0:T(8,128)(2,1)S(1)} %copy-done.6, ...), custom_call_target="tpu_custom_call" | custom-call | flops 16957440 | bytes 6838280 | tf_op jit(solution)/shard_map/middle_bwd/pallas_call | solution.py:29
  202.5 12.8 %attn_bwd.2 = (bf16[736,1152]{1,0:T(8,128)(2,1)S(1)}, bf16[368,1152]{1,0:T(8,128)(2,1)S(1)}, bf16[368,1152]{1,0:T(8,128)(2,1)S(1)}, f32[1,1152]{1,0:T(1,128)S(1)}) custom-call(s32[2]{0:T(128)S(1)} %get-tuple-element.244.sc_ref, bf16[368,1152]{1,0:T(8,128)(2,1)} %get-tuple-element.150.ga_ref.refs_4_, ...), custom_call_target="tpu_custom_call" | custom-call | flops 9098231808 | bytes 9465352 | tf_op jit(solution)/shard_map/attn_bwd/pallas_call | solution.py:29
  215.4 4.9 %collective-permute-done.29.far_ref = bf16[368,1152]{1,0:T(8,128)(2,1)S(1)} collective-permute-done((bf16[368,1152]{1,0:T(8,128)(2,1)S(1)}, bf16[368,1152]{1,0:T(8,128)(2,1)S(1)}, u32[]{:S(2)}, u32[]{:S(2)}) %collective-permute-start.29) | collective-permute-done | bytes 847904 | tf_op jit(solution)/shard_map/ppermute | solution.py:546
  226.2 11.7 %attn_bwd.3 = (bf16[736,1152]{1,0:T(8,128)(2,1)S(1)}, bf16[368,1152]{1,0:T(8,128)(2,1)S(1)}, bf16[368,1152]{1,0:T(8,128)(2,1)S(1)}, f32[1,1152]{1,0:T(1,128)S(1)}) custom-call(s32[2]{0:T(128)S(1)} %get-tuple-element.245.sc_ref, bf16[368,1152]{1,0:T(8,128)(2,1)S(1)} %get-tuple-element.161.ga_ref.refs_7_, ...), custom_call_target="tpu_custom_call" | custom-call | flops 9098231808 | bytes 9465352 | tf_op jit(solution)/shard_map/attn_bwd/pallas_call | solution.py:29
  239.9 8.6 %attn_dw.1 = bf16[1152,1152]{1,0:T(8,128)(2,1)S(1)} custom-call(bf16[736,1152]{1,0:T(8,128)(2,1)S(1)} %copy-done.41, bf16[736,1152]{1,0:T(8,128)(2,1)S(1)} %get-tuple-element.169.refs_1_, bf16[736,1152]{1,0:T(8,128)(2,1)S(1)} %copy-done.43, bf16[736,1152]{1,0:T(8,128)(2,1)S(1)} %get-tuple-element.171.refs_3_, ...), custom_call_target="tpu_custom_call" | custom-call | flops 4883742720 | bytes 13676544 | tf_op jit(solution)/shard_map/attn_dw/pallas_call | solution.py:29
  255.4 7.8 %collective-permute-done.32.far_ref = bf16[184,1152]{1,0:T(8,128)(2,1)S(1)} collective-permute-done((bf16[184,1152]{1,0:T(8,128)(2,1)S(1)}, bf16[184,1152]{1,0:T(8,128)(2,1)S(1)}, u32[]{:S(2)}, u32[]{:S(2)}) %collective-permute-start.32) | collective-permute-done | bytes 423968 | tf_op jit(solution)/shard_map/ppermute | solution.py:546
  273.0 11.5 %collective-permute-done.36 = f32[8564]{0:T(1024)S(1)} collective-permute-done((f32[8564]{0:T(1024)S(1)}, f32[8564]{0:T(1024)S(1)}, u32[]{:S(2)}, u32[]{:S(2)}) %collective-permute-start.36) | collective-permute-done | bytes 34288 | tf_op jit(solution)/shard_map/ppermute | solution.py:549
  286.3 4.6 %collective-permute-done.37 = f32[8564]{0:T(1024)S(1)} collective-permute-done((f32[8564]{0:T(1024)S(1)}, f32[8564]{0:T(1024)S(1)}, u32[]{:S(2)}, u32[]{:S(2)}) %collective-permute-start.37) | collective-permute-done | bytes 34288 | tf_op jit(solution)/shard_map/ppermute | solution.py:549
  292.3 3.9 %collective-permute-done.38 = f32[8564]{0:T(1024)S(1)} collective-permute-done((f32[8564]{0:T(1024)S(1)}, f32[8564]{0:T(1024)S(1)}, u32[]{:S(2)}, u32[]{:S(2)}) %collective-permute-start.38) | collective-permute-done | bytes 34288 | tf_op jit(solution)/shard_map/ppermute | solution.py:549
  296.8 3.8 %collective-permute-start.41 = (bf16[144,1152]{1,0:T(8,128)(2,1)S(1)}, bf16[144,1152]{1,0:T(8,128)(2,1)S(1)}, u32[]{:S(2)}, u32[]{:S(2)}) collective-permute-start(bf16[144,1152]{1,0:T(8,128)(2,1)S(1)} %get-tuple-element.184), channel_id=1, source_target_pairs={{0,24},{4,28},{8,0},{12,4},{16,8},{20,12},{24,16},{28,20},{1,25},{... | collective-permute-start | bytes 995336 | tf_op jit(solution)/shard_map/ppermute | solution.py:552
  305.7 3.7 %collective-permute-done.40.refs_2_ = bf16[144,1152]{1,0:T(8,128)(2,1)S(1)} collective-permute-done((bf16[144,1152]{1,0:T(8,128)(2,1)S(1)}, bf16[144,1152]{1,0:T(8,128)(2,1)S(1)}, u32[]{:S(2)}, u32[]{:S(2)}) %collective-permute-start.40) | collective-permute-done | bytes 331808 | tf_op jit(solution)/shard_map/ppermute | solution.py:552
  312.3 14.3 %collective-permute-done.42.refs_4_ = bf16[144,1152]{1,0:T(8,128)(2,1)S(1)} collective-permute-done((bf16[144,1152]{1,0:T(8,128)(2,1)S(1)}, bf16[144,1152]{1,0:T(8,128)(2,1)S(1)}, u32[]{:S(2)}, u32[]{:S(2)}) %collective-permute-start.42) | collective-permute-done | bytes 331808 | tf_op jit(solution)/shard_map/ppermute | solution.py:552
  (257 shorter events, 107.3 us)
Async XLA Ops:
  7.2 115.8 %all-gather.2.cloned.1.call-start = ((), (), s32[]{:S(2)}) async-start(), calls=%async_computation.1 | async-start | bytes 5640192 | tf_op jit(solution)/shard_map/all_gather | solution.py:615
  7.2 25.7 %collective-permute-start.3 = (bf16[2,184,1152]{2,1,0:T(8,128)(2,1)}, bf16[2,184,1152]{2,1,0:T(8,128)(2,1)S(1)}, u32[]{:S(2)}, u32[]{:S(2)}) collective-permute-start(bf16[2,184,1152]{2,1,0:T(8,128)(2,1)} %xo.11), channel_id=1, source_target_pairs={{0,2},{1,3},{2,0},{3,1},{4,6},{5,7},{6,4},{7,5},{8,10},{9,11},{10,... | collective-permute-start | bytes 2543624 | tf_op jit(solution)/shard_map/ppermute | solution.py:546
  15.8 17.2 %collective-permute-start.1 = (bf16[152,1152]{1,0:T(8,128)(2,1)}, bf16[152,1152]{1,0:T(8,128)(2,1)}, u32[]{:S(2)}, u32[]{:S(2)}) collective-permute-start(bf16[152,1152]{1,0:T(8,128)(2,1)} %pack_attn.1.refs_0_), channel_id=1, source_target_pairs={{0,24},{4,28},{8,0},{12,4},{16,8},{20,12},{24,16},{28,20},{1,25},{... | collective-permute-start | bytes 1050632 | tf_op jit(solution)/shard_map/ppermute | solution.py:552
  33.0 269.0 %reduce-scatter.2.cloned.1.call-start = ((), (), s32[]{:S(2)}) async-start(), calls=%async_computation.2 | async-start | bytes 5640192 | tf_op jit(solution)/shard_map/reduce_scatter | solution.py:653
  33.1 36.0 %collective-permute-start.9 = (bf16[2,184,1152]{2,1,0:T(8,128)(2,1)S(1)}, bf16[2,184,1152]{2,1,0:T(8,128)(2,1)}, u32[]{:S(2)}, u32[]{:S(2)}) collective-permute-start(bf16[2,184,1152]{2,1,0:T(8,128)(2,1)S(1)} %copy-done.4), channel_id=1, source_target_pairs={{0,2},{1,3},{2,0},{3,1},{4,6},{5,7},{6,4},{7,5},{8,10},{9,11},{10,... | collective-permute-start | bytes 2543624 | tf_op jit(solution)/shard_map/ppermute | solution.py:546
  33.7 35.3 %collective-permute-start.6 = (bf16[152,1152]{1,0:T(8,128)(2,1)S(1)}, bf16[152,1152]{1,0:T(8,128)(2,1)}, u32[]{:S(2)}, u32[]{:S(2)}) collective-permute-start(bf16[152,1152]{1,0:T(8,128)(2,1)S(1)} %copy-done.13), channel_id=1, source_target_pairs={{0,16},{4,20},{8,24},{12,28},{16,0},{20,4},{24,8},{28,12},{1,17},{... | collective-permute-start | bytes 1050632 | tf_op jit(solution)/shard_map/ppermute | solution.py:552
  34.9 34.2 %collective-permute-start.7 = (bf16[152,1152]{1,0:T(8,128)(2,1)S(1)}, bf16[152,1152]{1,0:T(8,128)(2,1)}, u32[]{:S(2)}, u32[]{:S(2)}) collective-permute-start(bf16[152,1152]{1,0:T(8,128)(2,1)S(1)} %collective-permute-done.refs_1_), channel_id=1, source_target_pairs={{0,4},{4,0},{8,12},{12,8},{16,20},{20,16},{24,28},{28,24},{1,5},{5... | collective-permute-start | bytes 1050632 | tf_op jit(solution)/shard_map/ppermute | solution.py:549
  36.4 32.6 %collective-permute-start.8 = (bf16[152,1152]{1,0:T(8,128)(2,1)}, bf16[152,1152]{1,0:T(8,128)(2,1)}, u32[]{:S(2)}, u32[]{:S(2)}) collective-permute-start(bf16[152,1152]{1,0:T(8,128)(2,1)} %collective-permute-done.1.refs_2_), channel_id=1, source_target_pairs={{0,4},{4,0},{8,12},{12,8},{16,20},{20,16},{24,28},{28,24},{1,5},{5... | collective-permute-start | bytes 1050632 | tf_op jit(solution)/shard_map/ppermute | solution.py:549
  36.9 49.5 %collective-permute-start.4 = (bf16[2,184,1152]{2,1,0:T(8,128)(2,1)S(1)}, bf16[2,184,1152]{2,1,0:T(8,128)(2,1)}, u32[]{:S(2)}, u32[]{:S(2)}) collective-permute-start(bf16[2,184,1152]{2,1,0:T(8,128)(2,1)S(1)} %copy-done), channel_id=1, source_target_pairs={{0,1},{1,0},{2,3},{3,2},{4,5},{5,4},{6,7},{7,6},{8,9},{9,8},{10,11... | collective-permute-start | bytes 2543624 | tf_op jit(solution)/shard_map/ppermute | solution.py:546
  68.9 17.5 %collective-permute-start.5 = (bf16[2,184,1152]{2,1,0:T(8,128)(2,1)S(1)}, bf16[2,184,1152]{2,1,0:T(8,128)(2,1)}, u32[]{:S(2)}, u32[]{:S(2)}) collective-permute-start(bf16[2,184,1152]{2,1,0:T(8,128)(2,1)S(1)} %collective-permute-done.3.xf), channel_id=1, source_target_pairs={{0,1},{1,0},{2,3},{3,2},{4,5},{5,4},{6,7},{7,6},{8,9},{9,8},{10,11... | collective-permute-start | bytes 2543624 | tf_op jit(solution)/shard_map/ppermute | solution.py:546
  100.6 21.0 %collective-permute-start.12 = (bf16[368,1152]{1,0:T(8,128)(2,1)S(1)}, bf16[368,1152]{1,0:T(8,128)(2,1)S(1)}, u32[]{:S(2)}, u32[]{:S(2)}) collective-permute-start(bf16[368,1152]{1,0:T(8,128)(2,1)S(1)} %add_convert_fusion.3.chip_ref), channel_id=1, source_target_pairs={{0,2},{1,3},{2,0},{3,1},{4,6},{5,7},{6,4},{7,5},{8,10},{9,11},{10,... | collective-permute-start | bytes 2543624 | tf_op jit(solution)/shard_map/ppermute | solution.py:546
  129.6 21.3 %collective-permute-start.19 = (bf16[368,1152]{1,0:T(8,128)(2,1)S(1)}, bf16[368,1152]{1,0:T(8,128)(2,1)S(1)}, u32[]{:S(2)}, u32[]{:S(2)}) collective-permute-start(bf16[368,1152]{1,0:T(8,128)(2,1)S(1)} %add_convert_fusion.2.chip_ref), channel_id=1, source_target_pairs={{0,2},{1,3},{2,0},{3,1},{4,6},{5,7},{6,4},{7,5},{8,10},{9,11},{10,... | collective-permute-start | bytes 2543624 | tf_op jit(solution)/shard_map/ppermute | solution.py:546
  153.2 21.3 %collective-permute-start.24 = (bf16[368,1152]{1,0:T(8,128)(2,1)S(1)}, bf16[368,1152]{1,0:T(8,128)(2,1)S(1)}, u32[]{:S(2)}, u32[]{:S(2)}) collective-permute-start(bf16[368,1152]{1,0:T(8,128)(2,1)S(1)} %add_convert_fusion.1.chip_ref), channel_id=1, source_target_pairs={{0,2},{1,3},{2,0},{3,1},{4,6},{5,7},{6,4},{7,5},{8,10},{9,11},{10,... | collective-permute-start | bytes 2543624 | tf_op jit(solution)/shard_map/ppermute | solution.py:546
  197.0 26.6 %collective-permute-start.16 = (bf16[368,1152]{1,0:T(8,128)(2,1)}, bf16[368,1152]{1,0:T(8,128)(2,1)S(1)}, u32[]{:S(2)}, u32[]{:S(2)}) collective-permute-start(bf16[368,1152]{1,0:T(8,128)(2,1)} %copy-done.37), channel_id=1, source_target_pairs={{0,1},{1,0},{2,3},{3,2},{4,5},{5,4},{6,7},{7,6},{8,9},{9,8},{10,11... | collective-permute-start | bytes 2543624 | tf_op jit(solution)/shard_map/ppermute | solution.py:546
  197.3 27.8 %collective-permute-start.22 = (bf16[368,1152]{1,0:T(8,128)(2,1)}, bf16[368,1152]{1,0:T(8,128)(2,1)S(1)}, u32[]{:S(2)}, u32[]{:S(2)}) collective-permute-start(bf16[368,1152]{1,0:T(8,128)(2,1)} %copy-done.38), channel_id=1, source_target_pairs={{0,1},{1,0},{2,3},{3,2},{4,5},{5,4},{6,7},{7,6},{8,9},{9,8},{10,11... | collective-permute-start | bytes 2543624 | tf_op jit(solution)/shard_map/ppermute | solution.py:546
  199.4 20.9 %collective-permute-start.29 = (bf16[368,1152]{1,0:T(8,128)(2,1)S(1)}, bf16[368,1152]{1,0:T(8,128)(2,1)S(1)}, u32[]{:S(2)}, u32[]{:S(2)}) collective-permute-start(bf16[368,1152]{1,0:T(8,128)(2,1)S(1)} %add_convert_fusion.chip_ref), channel_id=1, source_target_pairs={{0,2},{1,3},{2,0},{3,1},{4,6},{5,7},{6,4},{7,5},{8,10},{9,11},{10,... | collective-permute-start | bytes 2543624 | tf_op jit(solution)/shard_map/ppermute | solution.py:546
  223.8 40.4 %collective-permute-start.17 = (bf16[184,1152]{1,0:T(8,128)(2,1)S(1)}, bf16[184,1152]{1,0:T(8,128)(2,1)S(1)}, u32[]{:S(2)}, u32[]{:S(2)}) collective-permute-start(bf16[184,1152]{1,0:T(8,128)(2,1)S(1)} %add_convert_fusion.9), channel_id=1, source_target_pairs={{0,2},{1,3},{2,0},{3,1},{4,6},{5,7},{6,4},{7,5},{8,10},{9,11},{10,... | collective-permute-start | bytes 1271816 | tf_op jit(solution)/shard_map/ppermute | solution.py:546
  225.3 38.9 %collective-permute-start.23 = (bf16[184,1152]{1,0:T(8,128)(2,1)S(1)}, bf16[184,1152]{1,0:T(8,128)(2,1)S(1)}, u32[]{:S(2)}, u32[]{:S(2)}) collective-permute-start(bf16[184,1152]{1,0:T(8,128)(2,1)S(1)} %add_convert_fusion.7), channel_id=1, source_target_pairs={{0,2},{1,3},{2,0},{3,1},{4,6},{5,7},{6,4},{7,5},{8,10},{9,11},{10,... | collective-permute-start | bytes 1271816 | tf_op jit(solution)/shard_map/ppermute | solution.py:546
  238.5 16.1 %collective-permute-start.27 = (bf16[184,1152]{1,0:T(8,128)(2,1)S(1)}, bf16[184,1152]{1,0:T(8,128)(2,1)S(1)}, u32[]{:S(2)}, u32[]{:S(2)}) collective-permute-start(bf16[184,1152]{1,0:T(8,128)(2,1)S(1)} %add_convert_fusion.5), channel_id=1, source_target_pairs={{0,2},{1,3},{2,0},{3,1},{4,6},{5,7},{6,4},{7,5},{8,10},{9,11},{10,... | collective-permute-start | bytes 1271816 | tf_op jit(solution)/shard_map/ppermute | solution.py:546
  251.5 33.1 %collective-permute-start.33 = (bf16[3,144,1152]{2,1,0:T(8,128)(2,1)}, bf16[3,144,1152]{2,1,0:T(8,128)(2,1)}, u32[]{:S(2)}, u32[]{:S(2)}) collective-permute-start(bf16[3,144,1152]{2,1,0:T(8,128)(2,1)} %pad_maximum_fusion.1), channel_id=1, source_target_pairs={{0,4},{4,0},{8,12},{12,8},{16,20},{20,16},{24,28},{28,24},{1,5},{5... | collective-permute-start | bytes 2985992 | tf_op jit(solution)/shard_map/ppermute | solution.py:549
  269.5 15.1 %collective-permute-start.36 = (f32[8564]{0:T(1024)S(1)}, f32[8564]{0:T(1024)S(1)}, u32[]{:S(2)}, u32[]{:S(2)}) collective-permute-start(f32[8564]{0:T(1024)S(1)} %concatenate.35), channel_id=1, source_target_pairs={{0,4},{4,0},{8,12},{12,8},{16,20},{20,16},{24,28},{28,24},{1,5},{5... | collective-permute-start | bytes 102776 | tf_op jit(solution)/shard_map/ppermute | solution.py:549
  273.0 32.7 %collective-permute-start.39 = (bf16[144,1152]{1,0:T(8,128)(2,1)S(1)}, bf16[144,1152]{1,0:T(8,128)(2,1)S(1)}, u32[]{:S(2)}, u32[]{:S(2)}) collective-permute-start(bf16[144,1152]{1,0:T(8,128)(2,1)S(1)} %copy-done.53), channel_id=1, source_target_pairs={{0,4},{4,0},{8,12},{12,8},{16,20},{20,16},{24,28},{28,24},{1,5},{5... | collective-permute-start | bytes 995336 | tf_op jit(solution)/shard_map/ppermute | solution.py:549
  296.8 15.4 %collective-permute-start.41 = (bf16[144,1152]{1,0:T(8,128)(2,1)S(1)}, bf16[144,1152]{1,0:T(8,128)(2,1)S(1)}, u32[]{:S(2)}, u32[]{:S(2)}) collective-permute-start(bf16[144,1152]{1,0:T(8,128)(2,1)S(1)} %get-tuple-element.184), channel_id=1, source_target_pairs={{0,24},{4,28},{8,0},{12,4},{16,8},{20,12},{24,16},{28,20},{1,25},{... | collective-permute-start | bytes 995336 | tf_op jit(solution)/shard_map/ppermute | solution.py:552
  300.7 25.9 %collective-permute-start.42 = (bf16[144,1152]{1,0:T(8,128)(2,1)S(1)}, bf16[144,1152]{1,0:T(8,128)(2,1)S(1)}, u32[]{:S(2)}, u32[]{:S(2)}) collective-permute-start(bf16[144,1152]{1,0:T(8,128)(2,1)S(1)} %get-tuple-element.185), channel_id=1, source_target_pairs={{0,16},{4,20},{8,24},{12,28},{16,0},{20,4},{24,8},{28,12},{1,17},{... | collective-permute-start | bytes 995336 | tf_op jit(solution)/shard_map/ppermute | solution.py:552
  (80 other events, 799.4 us)
Sparse Core Ops, SparseCore 0:
  33.1 89.5 all-gather.1
  188.8 107.6 reduce-scatter.1
where the time goes:
time: 338 us; the launch traced here: 335 us
  waiting for transfers between devices  125 us (37%)
  Pallas kernels  108 us (32%)
  starting transfers between devices  37.7 us (11%)
  local copies, waits for them, and re-layouts  37.5 us (11%)
  between operations  15 us (4%)
  other arithmetic  12.2 us (4%)
    pallas_call x17, Pallas kernels, call(): pl.pallas_call(body, out_shape=shapes, in_specs=specs, out_specs=[VM] * l...  106 us
    ppermute x6, waiting for transfers between devices, turn(): return lax.ppermute(x, 'fsdp', [(i, (i + 2 * k) % fs) for i in range(fs)])  61.9 us
    ppermute x28, waiting for transfers between devices, swap_tp(): return lax.ppermute(x, 'tp', [(i, i ^ k) for i in range(tp)])  33.8 us
    unnamed x121, local copies, waits for them, and re-layouts  29.9 us
    ppermute x9, waiting for transfers between devices, swap_fs(): return lax.ppermute(x, 'fsdp', [(i, i ^ k) for i in range(fs)])  29.3 us
    ppermute x28, starting transfers between devices, swap_tp(): return lax.ppermute(x, 'tp', [(i, i ^ k) for i in range(tp)])  18.5 us
    ppermute x9, starting transfers between devices, swap_fs(): return lax.ppermute(x, 'fsdp', [(i, i ^ k) for i in range(fs)])  10.2 us
    ppermute x6, starting transfers between devices, turn(): return lax.ppermute(x, 'fsdp', [(i, (i + 2 * k) % fs) for i in range(fs)])  8.9 us
  transfers between devices with their start and end apart: 45, of which 20 were waited for; matrix products, arithmetic and copies ran while one was open for 7% of the time, Pallas kernels for 29%

commit v1 on v0

--- a/solution.py
+++ b/solution.py
@@ -689,10 +689,10 @@
     flat = jnp.concatenate(
         [wide.reshape(-1), cols[0, hw : 2 * hw], cols[0, 3 * hw :], unit_sums[0]], 0
     )
-    step = 1
-    while step < fs:
+    step = fs // 2
+    while step:
         flat = flat + swap_fs(flat, step)
-        step *= 2
+        step //= 2
     parts, flat = scatter_sums(g_attn, flat)
     r_up = r_mlp[:, :units]
     r_down = jnp.concatenate([r_mlp[:, main + 128 :], r_mlp[:, units : 2 * units - main]], 1).T

time: 338 us -> 336 us (level)
  waiting for transfers between devices: 125 us -> 119 us
    ppermute x9, waiting for transfers between devices: 29.3 us -> 21.5 us  [swap_fs(): return lax.ppermute(x, 'fsdp', [(i, i ^ k) for i in range(fs)])]
where the time goes in v1:
time: 336 us; the launch traced here: 332 us
  waiting for transfers between devices  119 us (35%)
  Pallas kernels  108 us (32%)
  starting transfers between devices  39.8 us (12%)
  local copies, waits for them, and re-layouts  37.5 us (11%)
  between operations  15 us (4%)
  other arithmetic  12.2 us (4%)
    pallas_call x17, Pallas kernels, call(): pl.pallas_call(body, out_shape=shapes, in_specs=specs, out_specs=[VM] * l...  106 us
    ppermute x6, waiting for transfers between devices, turn(): return lax.ppermute(x, 'fsdp', [(i, (i + 2 * k) % fs) for i in range(fs)])  64.1 us
    ppermute x28, waiting for transfers between devices, swap_tp(): return lax.ppermute(x, 'tp', [(i, i ^ k) for i in range(tp)])  33.8 us
    unnamed x121, local copies, waits for them, and re-layouts  29.9 us
    ppermute x9, waiting for transfers between devices, swap_fs(): return lax.ppermute(x, 'fsdp', [(i, i ^ k) for i in range(fs)])  21.5 us
    ppermute x28, starting transfers between devices, swap_tp(): return lax.ppermute(x, 'tp', [(i, i ^ k) for i in range(tp)])  18.5 us
    ppermute x9, starting transfers between devices, swap_fs(): return lax.ppermute(x, 'fsdp', [(i, i ^ k) for i in range(fs)])  12.3 us
    ppermute x6, starting transfers between devices, turn(): return lax.ppermute(x, 'fsdp', [(i, (i + 2 * k) % fs) for i in range(fs)])  8.9 us
  transfers between devices with their start and end apart: 45, of which 20 were waited for; matrix products, arithmetic and copies ran while one was open for 7% of the time, Pallas kernels for 29%

profile of v1, /device:TPU:0, one launch (start us, length us, event | category | flops | bytes accessed | tf_op | source)
XLA Modules:
  0.0 331.9 jit_solution(13599793341208472405)
XLA Ops:
  7.2 3.0 collective-permute-start.3
  23.8 3.5 %collective-permute-done.refs_1_ = bf16[152,1152]{1,0:T(8,128)(2,1)S(1)} collective-permute-done((bf16[152,1152]{1,0:T(8,128)(2,1)}, bf16[152,1152]{1,0:T(8,128)(2,1)S(1)}, u32[]{:S(2)}, u32[]{:S(2)}) %collective-permute-start) | collective-permute-done | bytes 350240 | tf_op jit(solution)/shard_map/ppermute | solution.py:552
  27.4 5.6 %collective-permute-done.1.refs_2_ = bf16[152,1152]{1,0:T(8,128)(2,1)} collective-permute-done((bf16[152,1152]{1,0:T(8,128)(2,1)}, bf16[152,1152]{1,0:T(8,128)(2,1)}, u32[]{:S(2)}, u32[]{:S(2)}) %collective-permute-start.1) | collective-permute-done | bytes 350240 | tf_op jit(solution)/shard_map/ppermute | solution.py:552
  36.9 32.0 %collective-permute-done.6.refs_3_ = bf16[152,1152]{1,0:T(8,128)(2,1)} collective-permute-done((bf16[152,1152]{1,0:T(8,128)(2,1)S(1)}, bf16[152,1152]{1,0:T(8,128)(2,1)}, u32[]{:S(2)}, u32[]{:S(2)}) %collective-permute-start.6) | collective-permute-done | bytes 350240 | tf_op jit(solution)/shard_map/ppermute | solution.py:552
  72.8 9.2 %collective-permute-done.10.refs_7_ = bf16[152,1152]{1,0:T(8,128)(2,1)} collective-permute-done((bf16[152,1152]{1,0:T(8,128)(2,1)}, bf16[152,1152]{1,0:T(8,128)(2,1)}, u32[]{:S(2)}, u32[]{:S(2)}) %collective-permute-start.10) | collective-permute-done | bytes 350240 | tf_op jit(solution)/shard_map/ppermute | solution.py:549
  88.2 9.7 %attn_fwd.2 = (bf16[736,1152]{1,0:T(8,128)(2,1)S(1)}, bf16[736,1152]{1,0:T(8,128)(2,1)S(1)}, bf16[736,288]{1,0:T(8,128)(2,1)S(1)}, f32[8,736]{1,0:T(8,128)S(1)},...) custom-call(s32[2]{0:T(128)S(1)} %get-tuple-element.244.sc_ref, bf16[2,184,1152]{2,1,0:T(8,128)(2,1)S(1)} %copy-done, ...), custom_call_target="tpu_custom_call" | custom-call | flops 6879444992 | bytes 11621896 | tf_op jit(solution)/shard_map/attn_fwd/pallas_call | solution.py:29
  102.0 10.6 %attn_fwd.3 = (bf16[736,1152]{1,0:T(8,128)(2,1)S(1)}, bf16[736,1152]{1,0:T(8,128)(2,1)S(1)}, bf16[736,288]{1,0:T(8,128)(2,1)S(1)}, f32[8,736]{1,0:T(8,128)S(1)},...) custom-call(s32[2]{0:T(128)S(1)} %get-tuple-element.245.sc_ref, bf16[2,184,1152]{2,1,0:T(8,128)(2,1)S(1)} %copy-done, ...), custom_call_target="tpu_custom_call" | custom-call | flops 6879444992 | bytes 11621896 | tf_op jit(solution)/shard_map/attn_fwd/pallas_call | solution.py:29
  116.8 4.8 %collective-permute-done.12.far_ref = bf16[368,1152]{1,0:T(8,128)(2,1)S(1)} collective-permute-done((bf16[368,1152]{1,0:T(8,128)(2,1)S(1)}, bf16[368,1152]{1,0:T(8,128)(2,1)S(1)}, u32[]{:S(2)}, u32[]{:S(2)}) %collective-permute-start.12) | collective-permute-done | bytes 847904 | tf_op jit(solution)/shard_map/ppermute | solution.py:546
  131.0 13.0 %mlp.2 = (bf16[736,1076]{1,0:T(8,128)(2,1)S(1)}, bf16[736,1076]{1,0:T(8,128)(2,1)S(1)}, bf16[736,1152]{1,0:T(8,128)(2,1)S(1)}, bf16[368,1152]{1,0:T(8,128)(2,1)S...) custom-call(s32[2]{0:T(128)S(1)} %get-tuple-element.244.sc_ref, ...), custom_call_target="tpu_custom_call" | custom-call | flops 7298482176 | bytes 18364328 | tf_op jit(solution)/shard_map/mlp/pallas_call | solution.py:29
  144.2 6.7 %collective-permute-done.19.far_ref = bf16[368,1152]{1,0:T(8,128)(2,1)S(1)} collective-permute-done((bf16[368,1152]{1,0:T(8,128)(2,1)S(1)}, bf16[368,1152]{1,0:T(8,128)(2,1)S(1)}, u32[]{:S(2)}, u32[]{:S(2)}) %collective-permute-start.19) | collective-permute-done | bytes 847904 | tf_op jit(solution)/shard_map/ppermute | solution.py:546
  155.3 12.8 %mlp.3 = (bf16[736,1076]{1,0:T(8,128)(2,1)S(1)}, bf16[736,1076]{1,0:T(8,128)(2,1)S(1)}, bf16[736,1152]{1,0:T(8,128)(2,1)S(1)}, bf16[368,1152]{1,0:T(8,128)(2,1)S...) custom-call(s32[2]{0:T(128)S(1)} %get-tuple-element.245.sc_ref, ...), custom_call_target="tpu_custom_call" | custom-call | flops 7298482176 | bytes 18364328 | tf_op jit(solution)/shard_map/mlp/pallas_call | solution.py:29
  175.4 11.0 %mlp_dw.1 = bf16[1152,2176]{1,0:T(8,128)(2,1)S(1)} custom-call(bf16[368,1152]{1,0:T(8,128)(2,1)S(1)} %get-tuple-element.133.na_ref.n2a0, bf16[368,1152]{1,0:T(8,128)(2,1)S(1)} %collective-permute-done.13.nb_ref.n2b0, bf16[368,1152]{1,0:T(8,128)(2,1)S(1)} %get-tuple-element.141.na_ref.n2a1, bf16[368,1152]{1,0:T(8,128)(2,1)S(1)} %collective-permute-done.20.nb_ref.n2b1, ...), custom_call_target="tpu_custom_call" | custom-call | flops 7298482176 | bytes 18131968 | tf_op jit(solution)/shard_map/mlp_dw/pallas_call | solution.py:29
  191.1 3.5 %middle_bwd.2 = (f32[184,1152]{1,0:T(8,128)S(1)}, bf16[368,1152]{1,0:T(8,128)(2,1)}, f32[4,1152]{1,0:T(4,128)S(1)}) custom-call(s32[2]{0:T(128)S(1)} %get-tuple-element.244.sc_ref, bf16[2,184,1152]{2,1,0:T(8,128)(2,1)S(1)} %copy-done.4, bf16[2,184,1152]{2,1,0:T(8,128)(2,1)} %collective-permute-done.9.cf, bf16[368,1152]{1,0:T(8,128)(2,1)S(1)} %copy-done.6, ...), custom_call_target="tpu_custom_call" | custom-call | flops 16957440 | bytes 6838280 | tf_op jit(solution)/shard_map/middle_bwd/pallas_call | solution.py:29
  202.5 12.8 %attn_bwd.2 = (bf16[736,1152]{1,0:T(8,128)(2,1)S(1)}, bf16[368,1152]{1,0:T(8,128)(2,1)S(1)}, bf16[368,1152]{1,0:T(8,128)(2,1)S(1)}, f32[1,1152]{1,0:T(1,128)S(1)}) custom-call(s32[2]{0:T(128)S(1)} %get-tuple-element.244.sc_ref, bf16[368,1152]{1,0:T(8,128)(2,1)} %get-tuple-element.150.ga_ref.refs_4_, ...), custom_call_target="tpu_custom_call" | custom-call | flops 9098231808 | bytes 9465352 | tf_op jit(solution)/shard_map/attn_bwd/pallas_call | solution.py:29
  215.4 4.9 %collective-permute-done.29.far_ref = bf16[368,1152]{1,0:T(8,128)(2,1)S(1)} collective-permute-done((bf16[368,1152]{1,0:T(8,128)(2,1)S(1)}, bf16[368,1152]{1,0:T(8,128)(2,1)S(1)}, u32[]{:S(2)}, u32[]{:S(2)}) %collective-permute-start.29) | collective-permute-done | bytes 847904 | tf_op jit(solution)/shard_map/ppermute | solution.py:546
  226.2 11.7 %attn_bwd.3 = (bf16[736,1152]{1,0:T(8,128)(2,1)S(1)}, bf16[368,1152]{1,0:T(8,128)(2,1)S(1)}, bf16[368,1152]{1,0:T(8,128)(2,1)S(1)}, f32[1,1152]{1,0:T(1,128)S(1)}) custom-call(s32[2]{0:T(128)S(1)} %get-tuple-element.245.sc_ref, bf16[368,1152]{1,0:T(8,128)(2,1)S(1)} %get-tuple-element.161.ga_ref.refs_7_, ...), custom_call_target="tpu_custom_call" | custom-call | flops 9098231808 | bytes 9465352 | tf_op jit(solution)/shard_map/attn_bwd/pallas_call | solution.py:29
  239.9 8.6 %attn_dw.1 = bf16[1152,1152]{1,0:T(8,128)(2,1)S(1)} custom-call(bf16[736,1152]{1,0:T(8,128)(2,1)S(1)} %copy-done.41, bf16[736,1152]{1,0:T(8,128)(2,1)S(1)} %get-tuple-element.169.refs_1_, bf16[736,1152]{1,0:T(8,128)(2,1)S(1)} %copy-done.43, bf16[736,1152]{1,0:T(8,128)(2,1)S(1)} %get-tuple-element.171.refs_3_, ...), custom_call_target="tpu_custom_call" | custom-call | flops 4883742720 | bytes 13676544 | tf_op jit(solution)/shard_map/attn_dw/pallas_call | solution.py:29
  255.4 7.8 %collective-permute-done.32.far_ref = bf16[184,1152]{1,0:T(8,128)(2,1)S(1)} collective-permute-done((bf16[184,1152]{1,0:T(8,128)(2,1)S(1)}, bf16[184,1152]{1,0:T(8,128)(2,1)S(1)}, u32[]{:S(2)}, u32[]{:S(2)}) %collective-permute-start.32) | collective-permute-done | bytes 423968 | tf_op jit(solution)/shard_map/ppermute | solution.py:546
  273.0 4.0 %collective-permute-done.36 = f32[8564]{0:T(1024)S(1)} collective-permute-done((f32[8564]{0:T(1024)S(1)}, f32[8564]{0:T(1024)S(1)}, u32[]{:S(2)}, u32[]{:S(2)}) %collective-permute-start.36) | collective-permute-done | bytes 34288 | tf_op jit(solution)/shard_map/ppermute | solution.py:549
  277.1 6.8 %collective-permute-done.33 = bf16[3,144,1152]{2,1,0:T(8,128)(2,1)} collective-permute-done((bf16[3,144,1152]{2,1,0:T(8,128)(2,1)}, bf16[3,144,1152]{2,1,0:T(8,128)(2,1)}, u32[]{:S(2)}, u32[]{:S(2)}) %collective-permute-start.33) | collective-permute-done | bytes 995360 | tf_op jit(solution)/shard_map/ppermute | solution.py:549
  291.2 3.8 %collective-permute-start.41 = (bf16[144,1152]{1,0:T(8,128)(2,1)S(1)}, bf16[144,1152]{1,0:T(8,128)(2,1)S(1)}, u32[]{:S(2)}, u32[]{:S(2)}) collective-permute-start(bf16[144,1152]{1,0:T(8,128)(2,1)S(1)} %get-tuple-element.184), channel_id=1, source_target_pairs={{0,24},{4,28},{8,0},{12,4},{16,8},{20,12},{24,16},{28,20},{1,25},{... | collective-permute-start | bytes 995336 | tf_op jit(solution)/shard_map/ppermute | solution.py:552
  300.1 3.7 %collective-permute-done.40.refs_2_ = bf16[144,1152]{1,0:T(8,128)(2,1)S(1)} collective-permute-done((bf16[144,1152]{1,0:T(8,128)(2,1)S(1)}, bf16[144,1152]{1,0:T(8,128)(2,1)S(1)}, u32[]{:S(2)}, u32[]{:S(2)}) %collective-permute-start.40) | collective-permute-done | bytes 331808 | tf_op jit(solution)/shard_map/ppermute | solution.py:552
  303.7 4.1 %collective-permute-done.41.refs_3_ = bf16[144,1152]{1,0:T(8,128)(2,1)S(1)} collective-permute-done((bf16[144,1152]{1,0:T(8,128)(2,1)S(1)}, bf16[144,1152]{1,0:T(8,128)(2,1)S(1)}, u32[]{:S(2)}, u32[]{:S(2)}) %collective-permute-start.41) | collective-permute-done | bytes 331808 | tf_op jit(solution)/shard_map/ppermute | solution.py:552
  307.8 15.2 %collective-permute-done.42.refs_4_ = bf16[144,1152]{1,0:T(8,128)(2,1)S(1)} collective-permute-done((bf16[144,1152]{1,0:T(8,128)(2,1)S(1)}, bf16[144,1152]{1,0:T(8,128)(2,1)S(1)}, u32[]{:S(2)}, u32[]{:S(2)}) %collective-permute-start.42) | collective-permute-done | bytes 331808 | tf_op jit(solution)/shard_map/ppermute | solution.py:552
  (257 shorter events, 108.0 us)
Async XLA Ops:
  7.2 115.8 %all-gather.2.cloned.1.call-start = ((), (), s32[]{:S(2)}) async-start(), calls=%async_computation.1 | async-start | bytes 5640192 | tf_op jit(solution)/shard_map/all_gather | solution.py:615
  7.2 25.7 %collective-permute-start.3 = (bf16[2,184,1152]{2,1,0:T(8,128)(2,1)}, bf16[2,184,1152]{2,1,0:T(8,128)(2,1)S(1)}, u32[]{:S(2)}, u32[]{:S(2)}) collective-permute-start(bf16[2,184,1152]{2,1,0:T(8,128)(2,1)} %xo.11), channel_id=1, source_target_pairs={{0,2},{1,3},{2,0},{3,1},{4,6},{5,7},{6,4},{7,5},{8,10},{9,11},{10,... | collective-permute-start | bytes 2543624 | tf_op jit(solution)/shard_map/ppermute | solution.py:546
  15.8 17.2 %collective-permute-start.1 = (bf16[152,1152]{1,0:T(8,128)(2,1)}, bf16[152,1152]{1,0:T(8,128)(2,1)}, u32[]{:S(2)}, u32[]{:S(2)}) collective-permute-start(bf16[152,1152]{1,0:T(8,128)(2,1)} %pack_attn.1.refs_0_), channel_id=1, source_target_pairs={{0,24},{4,28},{8,0},{12,4},{16,8},{20,12},{24,16},{28,20},{1,25},{... | collective-permute-start | bytes 1050632 | tf_op jit(solution)/shard_map/ppermute | solution.py:552
  18.0 14.9 %collective-permute-start.2 = (bf16[152,1152]{1,0:T(8,128)(2,1)}, bf16[152,1152]{1,0:T(8,128)(2,1)}, u32[]{:S(2)}, u32[]{:S(2)}) collective-permute-start(bf16[152,1152]{1,0:T(8,128)(2,1)} %pack_attn.1.refs_0_), channel_id=1, source_target_pairs={{0,4},{4,0},{8,12},{12,8},{16,20},{20,16},{24,28},{28,24},{1,5},{5... | collective-permute-start | bytes 1050632 | tf_op jit(solution)/shard_map/ppermute | solution.py:549
  33.0 263.3 %reduce-scatter.2.cloned.1.call-start = ((), (), s32[]{:S(2)}) async-start(), calls=%async_computation.2 | async-start | bytes 5640192 | tf_op jit(solution)/shard_map/reduce_scatter | solution.py:653
  33.1 36.0 %collective-permute-start.9 = (bf16[2,184,1152]{2,1,0:T(8,128)(2,1)S(1)}, bf16[2,184,1152]{2,1,0:T(8,128)(2,1)}, u32[]{:S(2)}, u32[]{:S(2)}) collective-permute-start(bf16[2,184,1152]{2,1,0:T(8,128)(2,1)S(1)} %copy-done.4), channel_id=1, source_target_pairs={{0,2},{1,3},{2,0},{3,1},{4,6},{5,7},{6,4},{7,5},{8,10},{9,11},{10,... | collective-permute-start | bytes 2543624 | tf_op jit(solution)/shard_map/ppermute | solution.py:546
  33.7 35.3 %collective-permute-start.6 = (bf16[152,1152]{1,0:T(8,128)(2,1)S(1)}, bf16[152,1152]{1,0:T(8,128)(2,1)}, u32[]{:S(2)}, u32[]{:S(2)}) collective-permute-start(bf16[152,1152]{1,0:T(8,128)(2,1)S(1)} %copy-done.13), channel_id=1, source_target_pairs={{0,16},{4,20},{8,24},{12,28},{16,0},{20,4},{24,8},{28,12},{1,17},{... | collective-permute-start | bytes 1050632 | tf_op jit(solution)/shard_map/ppermute | solution.py:552
  34.9 34.2 %collective-permute-start.7 = (bf16[152,1152]{1,0:T(8,128)(2,1)S(1)}, bf16[152,1152]{1,0:T(8,128)(2,1)}, u32[]{:S(2)}, u32[]{:S(2)}) collective-permute-start(bf16[152,1152]{1,0:T(8,128)(2,1)S(1)} %collective-permute-done.refs_1_), channel_id=1, source_target_pairs={{0,4},{4,0},{8,12},{12,8},{16,20},{20,16},{24,28},{28,24},{1,5},{5... | collective-permute-start | bytes 1050632 | tf_op jit(solution)/shard_map/ppermute | solution.py:549
  36.4 32.6 %collective-permute-start.8 = (bf16[152,1152]{1,0:T(8,128)(2,1)}, bf16[152,1152]{1,0:T(8,128)(2,1)}, u32[]{:S(2)}, u32[]{:S(2)}) collective-permute-start(bf16[152,1152]{1,0:T(8,128)(2,1)} %collective-permute-done.1.refs_2_), channel_id=1, source_target_pairs={{0,4},{4,0},{8,12},{12,8},{16,20},{20,16},{24,28},{28,24},{1,5},{5... | collective-permute-start | bytes 1050632 | tf_op jit(solution)/shard_map/ppermute | solution.py:549
  36.9 49.5 %collective-permute-start.4 = (bf16[2,184,1152]{2,1,0:T(8,128)(2,1)S(1)}, bf16[2,184,1152]{2,1,0:T(8,128)(2,1)}, u32[]{:S(2)}, u32[]{:S(2)}) collective-permute-start(bf16[2,184,1152]{2,1,0:T(8,128)(2,1)S(1)} %copy-done), channel_id=1, source_target_pairs={{0,1},{1,0},{2,3},{3,2},{4,5},{5,4},{6,7},{7,6},{8,9},{9,8},{10,11... | collective-permute-start | bytes 2543624 | tf_op jit(solution)/shard_map/ppermute | solution.py:546
  68.9 17.5 %collective-permute-start.5 = (bf16[2,184,1152]{2,1,0:T(8,128)(2,1)S(1)}, bf16[2,184,1152]{2,1,0:T(8,128)(2,1)}, u32[]{:S(2)}, u32[]{:S(2)}) collective-permute-start(bf16[2,184,1152]{2,1,0:T(8,128)(2,1)S(1)} %collective-permute-done.3.xf), channel_id=1, source_target_pairs={{0,1},{1,0},{2,3},{3,2},{4,5},{5,4},{6,7},{7,6},{8,9},{9,8},{10,11... | collective-permute-start | bytes 2543624 | tf_op jit(solution)/shard_map/ppermute | solution.py:546
  100.6 21.0 %collective-permute-start.12 = (bf16[368,1152]{1,0:T(8,128)(2,1)S(1)}, bf16[368,1152]{1,0:T(8,128)(2,1)S(1)}, u32[]{:S(2)}, u32[]{:S(2)}) collective-permute-start(bf16[368,1152]{1,0:T(8,128)(2,1)S(1)} %add_convert_fusion.3.chip_ref), channel_id=1, source_target_pairs={{0,2},{1,3},{2,0},{3,1},{4,6},{5,7},{6,4},{7,5},{8,10},{9,11},{10,... | collective-permute-start | bytes 2543624 | tf_op jit(solution)/shard_map/ppermute | solution.py:546
  129.6 21.3 %collective-permute-start.19 = (bf16[368,1152]{1,0:T(8,128)(2,1)S(1)}, bf16[368,1152]{1,0:T(8,128)(2,1)S(1)}, u32[]{:S(2)}, u32[]{:S(2)}) collective-permute-start(bf16[368,1152]{1,0:T(8,128)(2,1)S(1)} %add_convert_fusion.2.chip_ref), channel_id=1, source_target_pairs={{0,2},{1,3},{2,0},{3,1},{4,6},{5,7},{6,4},{7,5},{8,10},{9,11},{10,... | collective-permute-start | bytes 2543624 | tf_op jit(solution)/shard_map/ppermute | solution.py:546
  153.2 21.3 %collective-permute-start.24 = (bf16[368,1152]{1,0:T(8,128)(2,1)S(1)}, bf16[368,1152]{1,0:T(8,128)(2,1)S(1)}, u32[]{:S(2)}, u32[]{:S(2)}) collective-permute-start(bf16[368,1152]{1,0:T(8,128)(2,1)S(1)} %add_convert_fusion.1.chip_ref), channel_id=1, source_target_pairs={{0,2},{1,3},{2,0},{3,1},{4,6},{5,7},{6,4},{7,5},{8,10},{9,11},{10,... | collective-permute-start | bytes 2543624 | tf_op jit(solution)/shard_map/ppermute | solution.py:546
  197.0 26.6 %collective-permute-start.16 = (bf16[368,1152]{1,0:T(8,128)(2,1)}, bf16[368,1152]{1,0:T(8,128)(2,1)S(1)}, u32[]{:S(2)}, u32[]{:S(2)}) collective-permute-start(bf16[368,1152]{1,0:T(8,128)(2,1)} %copy-done.37), channel_id=1, source_target_pairs={{0,1},{1,0},{2,3},{3,2},{4,5},{5,4},{6,7},{7,6},{8,9},{9,8},{10,11... | collective-permute-start | bytes 2543624 | tf_op jit(solution)/shard_map/ppermute | solution.py:546
  197.3 27.8 %collective-permute-start.22 = (bf16[368,1152]{1,0:T(8,128)(2,1)}, bf16[368,1152]{1,0:T(8,128)(2,1)S(1)}, u32[]{:S(2)}, u32[]{:S(2)}) collective-permute-start(bf16[368,1152]{1,0:T(8,128)(2,1)} %copy-done.38), channel_id=1, source_target_pairs={{0,1},{1,0},{2,3},{3,2},{4,5},{5,4},{6,7},{7,6},{8,9},{9,8},{10,11... | collective-permute-start | bytes 2543624 | tf_op jit(solution)/shard_map/ppermute | solution.py:546
  199.4 20.9 %collective-permute-start.29 = (bf16[368,1152]{1,0:T(8,128)(2,1)S(1)}, bf16[368,1152]{1,0:T(8,128)(2,1)S(1)}, u32[]{:S(2)}, u32[]{:S(2)}) collective-permute-start(bf16[368,1152]{1,0:T(8,128)(2,1)S(1)} %add_convert_fusion.chip_ref), channel_id=1, source_target_pairs={{0,2},{1,3},{2,0},{3,1},{4,6},{5,7},{6,4},{7,5},{8,10},{9,11},{10,... | collective-permute-start | bytes 2543624 | tf_op jit(solution)/shard_map/ppermute | solution.py:546
  223.8 40.4 %collective-permute-start.17 = (bf16[184,1152]{1,0:T(8,128)(2,1)S(1)}, bf16[184,1152]{1,0:T(8,128)(2,1)S(1)}, u32[]{:S(2)}, u32[]{:S(2)}) collective-permute-start(bf16[184,1152]{1,0:T(8,128)(2,1)S(1)} %add_convert_fusion.9), channel_id=1, source_target_pairs={{0,2},{1,3},{2,0},{3,1},{4,6},{5,7},{6,4},{7,5},{8,10},{9,11},{10,... | collective-permute-start | bytes 1271816 | tf_op jit(solution)/shard_map/ppermute | solution.py:546
  225.3 38.9 %collective-permute-start.23 = (bf16[184,1152]{1,0:T(8,128)(2,1)S(1)}, bf16[184,1152]{1,0:T(8,128)(2,1)S(1)}, u32[]{:S(2)}, u32[]{:S(2)}) collective-permute-start(bf16[184,1152]{1,0:T(8,128)(2,1)S(1)} %add_convert_fusion.7), channel_id=1, source_target_pairs={{0,2},{1,3},{2,0},{3,1},{4,6},{5,7},{6,4},{7,5},{8,10},{9,11},{10,... | collective-permute-start | bytes 1271816 | tf_op jit(solution)/shard_map/ppermute | solution.py:546
  238.5 16.1 %collective-permute-start.27 = (bf16[184,1152]{1,0:T(8,128)(2,1)S(1)}, bf16[184,1152]{1,0:T(8,128)(2,1)S(1)}, u32[]{:S(2)}, u32[]{:S(2)}) collective-permute-start(bf16[184,1152]{1,0:T(8,128)(2,1)S(1)} %add_convert_fusion.5), channel_id=1, source_target_pairs={{0,2},{1,3},{2,0},{3,1},{4,6},{5,7},{6,4},{7,5},{8,10},{9,11},{10,... | collective-permute-start | bytes 1271816 | tf_op jit(solution)/shard_map/ppermute | solution.py:546
  251.5 32.4 %collective-permute-start.33 = (bf16[3,144,1152]{2,1,0:T(8,128)(2,1)}, bf16[3,144,1152]{2,1,0:T(8,128)(2,1)}, u32[]{:S(2)}, u32[]{:S(2)}) collective-permute-start(bf16[3,144,1152]{2,1,0:T(8,128)(2,1)} %pad_maximum_fusion.1), channel_id=1, source_target_pairs={{0,4},{4,0},{8,12},{12,8},{16,20},{20,16},{24,28},{28,24},{1,5},{5... | collective-permute-start | bytes 2985992 | tf_op jit(solution)/shard_map/ppermute | solution.py:549
  271.1 29.0 %collective-permute-start.39 = (bf16[144,1152]{1,0:T(8,128)(2,1)S(1)}, bf16[144,1152]{1,0:T(8,128)(2,1)S(1)}, u32[]{:S(2)}, u32[]{:S(2)}) collective-permute-start(bf16[144,1152]{1,0:T(8,128)(2,1)S(1)} %copy-done.53), channel_id=1, source_target_pairs={{0,4},{4,0},{8,12},{12,8},{16,20},{20,16},{24,28},{28,24},{1,5},{5... | collective-permute-start | bytes 995336 | tf_op jit(solution)/shard_map/ppermute | solution.py:549
  291.2 16.6 %collective-permute-start.41 = (bf16[144,1152]{1,0:T(8,128)(2,1)S(1)}, bf16[144,1152]{1,0:T(8,128)(2,1)S(1)}, u32[]{:S(2)}, u32[]{:S(2)}) collective-permute-start(bf16[144,1152]{1,0:T(8,128)(2,1)S(1)} %get-tuple-element.184), channel_id=1, source_target_pairs={{0,24},{4,28},{8,0},{12,4},{16,8},{20,12},{24,16},{28,20},{1,25},{... | collective-permute-start | bytes 995336 | tf_op jit(solution)/shard_map/ppermute | solution.py:552
  295.0 28.0 %collective-permute-start.42 = (bf16[144,1152]{1,0:T(8,128)(2,1)S(1)}, bf16[144,1152]{1,0:T(8,128)(2,1)S(1)}, u32[]{:S(2)}, u32[]{:S(2)}) collective-permute-start(bf16[144,1152]{1,0:T(8,128)(2,1)S(1)} %get-tuple-element.185), channel_id=1, source_target_pairs={{0,16},{4,20},{8,24},{12,28},{16,0},{20,4},{24,8},{28,12},{1,17},{... | collective-permute-start | bytes 995336 | tf_op jit(solution)/shard_map/ppermute | solution.py:552
  (80 other events, 789.3 us)
Sparse Core Ops, SparseCore 0:
  33.1 89.5 all-gather.1
  188.8 106.4 reduce-scatter.1
